TPU v7x, 32 devices: a whole 2x2x4 slice. The times are simulated.
32 devices in a mesh: dp: 4 (over y, x), expert: 8 (over z, core).
Axes of the slice: x: 2, y: 2, z: 4, core: 2. Of those that a mesh axis runs over, the one named last changes fastest.
Arguments:
- item_feats: bfloat16 [8, 2048, 256], P('expert', 'dp'), may hold values from -6 to 6
- expert_ids: int32 [8, 2048, 1], P('expert', 'dp'), may hold values from 0 to 31; in each aligned block of 512 rows (0 to 511, 512 to 1023, ..., all dimensions but the last counted through in order) at most 32 rows name the same one
- weight_in: bfloat16 [32, 256, 1024], P('expert'), may hold values from -0.375 to 0.375
- weight_out: bfloat16 [32, 1024, 256], P('expert'), may hold values from -0.1875 to 0.1875
- queries: bfloat16 [8, 2048, 256], P('expert', 'dp'), may hold values from -150 to 150
- query_weight: float32 [8, 2048], P('expert', 'dp'), may hold values from 0.25 to 2
- positives: int32 [8, 2048], P('expert', 'dp'), may hold values from 0 to 2047
- sample_counts: int32 [8, 2048], P('expert'), may hold values from 1 to 4095
Outputs:
- query_loss: float32 [8, 2048], P('expert', 'dp')
- grad_queries: float32 [8, 2048, 256], P('expert', 'dp')
- grad_items: float32 [8, 2048, 256], P('expert', 'dp')
- grad_weight_in: float32 [256, 32, 1024], P('dp', 'expert')
- grad_weight_out: float32 [1024, 32, 256], P('dp', 'expert')
Inputs may be any that keep to these rules, and one draw needn't show every extreme that they name: `expert_ids`: the 512 items of one device name each expert at most 32 times.
All inputs are finite; a program needn't handle non-finite values.
Results may differ from a plain program's by a relative error of at most 0.023.
The roundings to bfloat16 on the way count: a program that leaves them out, or rounds other values in their place, can miss the bound.
Values may be sent and summed in bfloat16 or wider, within the bound.
No kernel may reach another device: no remote copies, remote signals or barrier semaphores. Data moves between devices by JAX's collectives and lax.ppermute only.
A program may use at most 128 MiB of HBM per device.

v0:
```python
import jax
import jax.numpy as jnp
from jax import lax
from jax.sharding import PartitionSpec as P

CAP = 32
norm_eps = 1e-06


def per_device(
    item_feats, expert_ids, weight_in, weight_out, queries, query_weight, positives, sample_counts
):
    groups = lax.axis_size("expert")
    shards = lax.axis_size("dp")
    local_experts = weight_in.shape[0]
    experts_all = local_experts * groups
    item_rows = item_feats.shape[1]
    feat_width = item_feats.shape[2]
    query_rows = queries.shape[1]
    slots_per = CAP
    features = item_feats[0].astype(jnp.float32)
    routes = expert_ids[0, :, 0]
    inv_rms = lax.rsqrt(jnp.mean(features * features, axis=1, keepdims=True) + norm_eps)
    normed = (features * inv_rms).astype(jnp.bfloat16)
    onehot = (routes[:, None] == jnp.arange(experts_all, dtype=jnp.int32)[None, :]).astype(
        jnp.int32
    )
    before = jnp.cumsum(onehot, axis=0) - onehot
    places = routes * slots_per + jnp.sum(before * onehot, axis=1)

    def scatter_slots(values):
        empty = jnp.zeros((experts_all * slots_per, feat_width), jnp.bfloat16)
        return empty.at[places].set(values).reshape(groups, local_experts, slots_per, feat_width)

    expert_received = lax.all_to_all(
        scatter_slots(normed), "expert", split_axis=0, concat_axis=0, tiled=True
    )
    hidden = jnp.einsum(
        "skcd,kdf->skcf", expert_received, weight_in, preferred_element_type=jnp.float32
    )
    expert_active = jax.nn.gelu(hidden).astype(jnp.bfloat16)
    output = jnp.einsum(
        "skcf,kfd->skcd", expert_active, weight_out, preferred_element_type=jnp.float32
    ).astype(jnp.bfloat16)
    output, received, active, hidden = (output, expert_received, expert_active, hidden)
    returned = lax.all_to_all(output, "expert", split_axis=0, concat_axis=0, tiled=True)
    branch = returned.reshape(experts_all * slots_per, feat_width)[places].astype(jnp.float32)
    reduced_sum = features + branch
    length = jnp.sqrt(jnp.sum(reduced_sum * reduced_sum, axis=1, keepdims=True) + norm_eps)
    unit_vecs = reduced_sum / length
    unit_low = unit_vecs.astype(jnp.bfloat16)
    query_matrix = queries[0]
    weights = query_weight[0]
    targets = positives[0]
    log_counts = jnp.log(sample_counts[0].astype(jnp.float32))
    shard_rows = lax.all_gather(unit_low, "dp", axis=0, tiled=True)
    running = jnp.full((query_rows,), -jnp.inf, jnp.float32)
    totals = jnp.zeros((query_rows,), jnp.float32)
    row_count = shard_rows.shape[0]
    scores = (
        jnp.einsum("qd,kd->qk", query_matrix, shard_rows, preferred_element_type=jnp.float32)
        - log_counts[None, :]
    )
    highest = jnp.max(scores, axis=1)
    totals = totals * jnp.exp(running - highest) + jnp.sum(
        jnp.exp(scores - highest[:, None]), axis=1
    )
    columns = jnp.arange(row_count, dtype=jnp.int32)
    picked = jnp.sum(jnp.where(columns[None, :] == targets[:, None], scores, 0.0), axis=1)
    gathered, highest, totals, picked = (shard_rows, highest, totals, picked)
    log_total = highest + jnp.log(totals)
    query_loss = (log_total - picked)[None, :]
    block_layout = gathered.reshape(shards, item_rows, feat_width)
    counts_view = log_counts.reshape(shards, item_rows)

    def weigh_block(inputs):
        item_tile_rows, block_logs, first_item = inputs
        scores = (
            jnp.einsum(
                "qd,kd->qk", query_matrix, item_tile_rows, preferred_element_type=jnp.float32
            )
            - block_logs[None, :]
        )
        columns = first_item + jnp.arange(item_rows, dtype=jnp.int32)
        target_hit = (columns[None, :] == targets[:, None]).astype(jnp.float32)
        return (weights[:, None] * (jnp.exp(scores - log_total[:, None]) - target_hit)).astype(
            jnp.bfloat16
        )

    mixing_factors = lax.map(
        weigh_block, (block_layout, counts_view, jnp.arange(shards, dtype=jnp.int32) * item_rows)
    )
    grad_queries = jnp.einsum(
        "ira,ias->rs", mixing_factors, block_layout, preferred_element_type=jnp.float32
    )
    all_queries = lax.all_gather(query_matrix, "dp", axis=0, tiled=True)
    all_lse, all_weights, all_targets = (
        lax.all_gather(log_total, "dp", axis=0, tiled=True),
        lax.all_gather(weights, "dp", axis=0, tiled=True),
        lax.all_gather(targets.astype(jnp.float32), "dp", axis=0, tiled=True),
    )
    first_item = lax.axis_index("dp") * item_rows
    own_logs = lax.dynamic_slice_in_dim(log_counts, first_item, item_rows)
    scores = (
        jnp.einsum("qd,kd->qk", all_queries, unit_low, preferred_element_type=jnp.float32)
        - own_logs[None, :]
    )
    columns = first_item + jnp.arange(item_rows, dtype=jnp.int32)
    target_hit = (columns[None, :] == all_targets.astype(jnp.int32)[:, None]).astype(jnp.float32)
    terms = (all_weights[:, None] * (jnp.exp(scores - all_lse[:, None]) - target_hit)).astype(
        jnp.bfloat16
    )
    grad_unit = jnp.einsum("qk,qd->kd", terms, all_queries, preferred_element_type=jnp.float32)
    along = jnp.sum(unit_vecs * grad_unit, axis=1, keepdims=True)
    grad_summed = (grad_unit - unit_vecs * along) / length
    grad_low = grad_summed.astype(jnp.bfloat16)
    grad_in = lax.all_to_all(
        scatter_slots(grad_low), "expert", split_axis=0, concat_axis=0, tiled=True
    )
    grad_active = jnp.einsum(
        "skcd,kfd->skcf", grad_in, weight_out, preferred_element_type=jnp.float32
    )
    grad_hidden = jax.vjp(jax.nn.gelu, hidden)[1](grad_active)[0].astype(jnp.bfloat16)
    grad_normed = jnp.einsum(
        "skcf,kdf->skcd", grad_hidden, weight_in, preferred_element_type=jnp.float32
    ).astype(jnp.bfloat16)
    grad_back = lax.all_to_all(grad_normed, "expert", split_axis=0, concat_axis=0, tiled=True)
    grad_rows = grad_back.reshape(experts_all * slots_per, feat_width)[places].astype(jnp.float32)
    projected = jnp.mean(grad_rows * features, axis=1, keepdims=True)
    grad_items = grad_summed + inv_rms * (grad_rows - features * inv_rms * inv_rms * projected)
    cut_rows = received
    grad_weight_in = lax.psum_scatter(
        jnp.einsum(
            "skcr,skcf->rkf", cut_rows, grad_hidden, preferred_element_type=jnp.float32
        ).astype(jnp.bfloat16),
        "dp",
        scatter_dimension=0,
        tiled=True,
    ).astype(jnp.float32)
    cut_rows = active
    grad_weight_out = lax.psum_scatter(
        jnp.einsum("skcr,skcd->rkd", cut_rows, grad_in, preferred_element_type=jnp.float32).astype(
            jnp.bfloat16
        ),
        "dp",
        scatter_dimension=0,
        tiled=True,
    ).astype(jnp.float32)
    return (query_loss, grad_queries[None], grad_items[None], grad_weight_in, grad_weight_out)


def solution(mesh):
    placed = (
        P("expert", "dp", None),
        P("expert", "dp", None),
        P("expert", None, None),
        P("expert", None, None),
        P("expert", "dp", None),
        P("expert", "dp"),
        P("expert", "dp"),
        P("expert", None),
    )
    return jax.shard_map(
        per_device,
        mesh=mesh,
        in_specs=placed,
        out_specs=(
            P("expert", "dp"),
            P("expert", "dp", None),
            P("expert", "dp", None),
            P("dp", "expert", None),
            P("dp", "expert", None),
        ),
        check_vma=False,
    )
```

profile of v0, /device:TPU:0, one launch (start us, length us, event | category | flops | bytes accessed | tf_op | source)
XLA Modules:
  0.0 273.3 jit_solution(7844112702269613480)
XLA Ops:
  12.3 2.5 scatter_custom_fusion
  14.8 21.5 %all_to_all.20 = bf16[8,4,32,256]{3,2,1,0:T(8,128)(2,1)S(1)} all-to-all(bf16[8,4,32,256]{3,2,1,0:T(8,128)(2,1)S(1)} %bitcast.219), channel_id=1, replica_groups=mesh['dp'=4,'expert'=8] {'expert'}, dimensions={0} | all-to-all | bytes 1048576 | tf_op jit(solution)/shard_map/all_to_all | solution.py:35
  36.3 3.5 %fusion.26 = (bf16[8,4,32,1024]{3,2,0,1:T(8,128)(2,1)S(1)}, f32[4,8,32,1024]{3,2,1,0:T(8,128)}) fusion(bf16[4,256,1024]{2,1,0:T(8,128)(2,1)S(1)} %copy-done, bf16[8,4,32,256]{3,2,1,0:T(8,128)(2,1)S(1)} %all_to_all.20), kind=kOutput, calls=%fused_computation.43 | convolution fusion | flops 546308096 | bytes 8912896 | tf_op jit(solution)/shard_map/skcd,kdf->skcf/dot_general | solution.py:38
  42.0 3.5 %all-to-all-start.1 = ((bf16[8,4,32,256]{3,2,1,0:T(8,128)(2,1)}), bf16[8,4,32,256]{3,2,1,0:T(8,128)(2,1)S(1)}, u32[]{:S(2)}, u32[]{:S(2)}) async-start(bf16[8,4,32,256]{3,2,1,0:T(8,128)(2,1)} %copy.40), calls=%async_computation.1 | async-start | bytes 1048576 | tf_op jit(solution)/shard_map/all_to_all | solution.py:46
  45.5 15.2 %all-to-all-done.1 = bf16[8,4,32,256]{3,2,1,0:T(8,128)(2,1)S(1)} async-done(((bf16[8,4,32,256]{3,2,1,0:T(8,128)(2,1)}), bf16[8,4,32,256]{3,2,1,0:T(8,128)(2,1)S(1)}, u32[]{:S(2)}, u32[]{:S(2)}) %all-to-all-start.1) | async-done | bytes 524320 | tf_op jit(solution)/shard_map/all_to_all | solution.py:46
  64.6 8.1 %all-gather.3 = f32[4,1,512]{2,1,0:T(1,128)S(1)} all-gather(f32[1,1,512]{2,1,0:T(1,128)S(1)} %bitcast.239), channel_id=1, replica_groups=mesh['dp'=4,'expert'=8] {'dp'}, dimensions={0}, use_global_device_ids=true | all-gather | bytes 10240 | tf_op jit(solution)/shard_map/all_gather | solution.py:100
  72.7 8.1 %all-gather = f32[1,2048]{1,0:T(1,128)S(1)} all-gather(f32[1,512]{1,0:T(1,128)S(1)} %copy-done.13), channel_id=2, replica_groups=mesh['dp'=4,'expert'=8] {'dp'}, dimensions={1}, use_global_device_ids=true | all-gather | bytes 10240 | tf_op jit(solution)/shard_map/all_gather | solution.py:99
  80.9 8.4 %all-gather.7.cloned.1.call-done = bf16[2048,256]{0,1:T(8,128)(2,1)} async-done(((bf16[512,256]{0,1:T(8,128)(2,1)}), bf16[2048,256]{0,1:T(8,128)(2,1)}) %all-gather.7.cloned.1.call-update) | async-done | bytes 1048592 | tf_op jit(solution)/shard_map/all_gather | solution.py:56
  89.3 2.2 subtract_reduce_fusion
  92.8 8.2 %all-gather.2 = f32[4,1,512]{2,1,0:T(1,128)S(1)} all-gather(f32[1,1,512]{2,1,0:T(1,128)S(1)} %bitcast.232), channel_id=1, replica_groups=mesh['dp'=4,'expert'=8] {'dp'}, dimensions={0}, use_global_device_ids=true | all-gather | bytes 10240 | tf_op jit(solution)/shard_map/all_gather | solution.py:98
  101.0 16.6 %all-gather.9.cloned.1.call-done = bf16[1,2048,256]{2,1,0:T(8,128)(2,1)} async-done(((bf16[1,512,256]{2,1,0:T(8,128)(2,1)}), bf16[1,2048,256]{2,1,0:T(8,128)(2,1)}) %all-gather.9.cloned.1.call-update) | async-done | bytes 1048592 | tf_op jit(solution)/shard_map/all_gather | solution.py:96
  117.6 3.8 %multiply_reduce_fusion = (f32[512]{0:T(512)S(1)}, f32[512,256]{0,1:T(8,128)S(1)}) fusion(f32[512]{0:T(512)S(1)} %add_sqrt_fusion, bf16[512,256]{0,1:T(8,128)(2,1)S(1)} %copy.41, bf16[1,512,256]{1,2,0:T(8,128)(2,1)S(1)} %copy.36, bf16[1,2048,256]{2,1,0:T(8,128)(2,1)} %all-gather.9.cloned.1.call-done, bf16[512,256]{0,1:T(8,128)(2,1)S(1)} %copy-done.7, ...), kind=kOutput, calls=%fused_computation.80 | convolution fusion | flops 1081867776 | bytes 2392064 | tf_op jit(solution)/shard_map/qk,qd->kd/dot_general | solution.py:113
  121.7 3.1 %scatter_custom_fusion.1 = bf16[1024,256]{1,0:T(8,128)(2,1)} fusion(s32[512]{0:T(512)S(1)} %bitcast.235, bf16[512,256]{1,0:T(8,128)(2,1)S(1)} %copy.44, bf16[]{:T(256)} %constant.12.clone.1), kind=kCustom, calls=%fused_computation.85 | custom fusion | bytes 524290 | tf_op jit(solution)/shard_map/scatter | solution.py:33
  124.8 19.9 %all_to_all.21 = bf16[8,4,32,256]{3,2,1,0:T(8,128)(2,1)S(1)} all-to-all(bf16[8,4,32,256]{3,2,1,0:T(8,128)(2,1)} %bitcast.218), channel_id=1, replica_groups=mesh['dp'=4,'expert'=8] {'expert'}, dimensions={0} | all-to-all | bytes 1048576 | tf_op jit(solution)/shard_map/all_to_all | solution.py:117
  144.8 5.9 %fusion.17 = bf16[8,4,32,1024]{3,2,0,1:T(8,128)(2,1)S(1)} fusion(f32[4,8,32,1024]{3,2,1,0:T(8,128)} %get-tuple-element.91, bf16[4,1024,256]{2,1,0:T(8,128)(2,1)} %param.13, bf16[8,4,32,256]{3,2,1,0:T(8,128)(2,1)S(1)} %all_to_all.21), kind=kOutput, calls=%fused_computation.26 | convolution fusion | flops 557842432 | bytes 8912896 | tf_op jit(solution)/shard_map/skcd,kfd->skcf/dot_general | solution.py:120
  152.1 2.2 fusion.35
  154.3 4.6 %copy.49 = bf16[256,4,1024]{2,1,0:T(4,128)(2,1)} copy(bf16[256,4,1024]{0,2,1:T(8,128)(2,1)} %fusion.35) | data formatting | bytes 4194304 | tf_op jit(solution)/shard_map/convert_element_type | solution.py:135
  159.0 3.9 %fusion.36 = bf16[1024,4,256]{0,2,1:T(8,128)(2,1)} fusion(bf16[8,4,32,256]{3,2,1,0:T(8,128)(2,1)} %copy-done.10, bf16[8,4,32,1024]{3,2,0,1:T(8,128)(2,1)} %copy-done.16), kind=kOutput, calls=%fused_computation.55 | convolution fusion | flops 537919488 | bytes 4718592 | tf_op jit(solution)/shard_map/skcr,skcd->rkd/dot_general | solution.py:142
  165.5 2.4 fusion.45
  168.7 3.7 %all-to-all-start.3 = ((bf16[8,4,32,256]{3,2,1,0:T(8,128)(2,1)}), bf16[8,4,32,256]{3,2,1,0:T(8,128)(2,1)S(1)}, u32[]{:S(2)}, u32[]{:S(2)}) async-start(bf16[8,4,32,256]{3,2,1,0:T(8,128)(2,1)} %copy.46), calls=%async_computation.3 | async-start | bytes 1048576 | tf_op jit(solution)/shard_map/all_to_all | solution.py:127
  172.5 14.0 %while.10 = (s32[]{:T(128)}, bf16[4,512,512]{1,2,0:T(8,128)(2,1)}, f32[1,512]{1,0:T(1,128)S(1)}, bf16[4,512,256]{2,1,0:T(8,128)(2,1)}, bf16[512,256]{1,0:T(8,128...) while((s32[]{:T(128)}, bf16[4,512,512]{1,2,0:T(8,128)(2,1)}, ...), condition=%wide.region_10.11_spmd, body=%wide.region_9.10_spmd.sunk | while | flops 136053248 | bytes 1066105 | solution.py:90
  173.7 2.2 fusion.97
  177.2 2.2 fusion.97
  180.7 2.2 fusion.97
  184.2 2.2 fusion.97
  187.1 3.4 %convolution_bitcast_fusion = f32[1,512,256]{2,1,0:T(8,128)} fusion(bf16[4,512,512]{1,2,0:T(8,128)(2,1)} %get-tuple-element.52, bf16[4,512,256]{2,1,0:T(8,128)(2,1)} %get-tuple-element.190), kind=kOutput, calls=%fused_computation.60 | convolution fusion | flops 536870912 | bytes 3670016 | tf_op jit(solution)/shard_map/ira,ias->rs/dot_general | solution.py:93
  192.7 2.1 fusion.61
  194.8 2.0 copy.51
  196.8 29.7 %all-reduce.3.cloned.1.call-done = bf16[256,4,1024]{2,1,0:T(4,128)(2,1)} async-done(((bf16[256,4,1024]{2,1,0:T(4,128)(2,1)}), bf16[256,4,1024]{2,1,0:T(4,128)(2,1)}) %all-reduce.3.cloned.1.call-update) | async-done | bytes 2097168
  226.5 2.2 dynamic-slice_convert_fusion
  228.6 35.9 %reduce-scatter.2.cloned.1.call-done = bf16[256,4,256]{0,2,1:T(8,128)(2,1)} async-done(((bf16[1024,4,256]{0,2,1:T(8,128)(2,1)}), bf16[256,4,256]{0,2,1:T(8,128)(2,1)}) %reduce-scatter.2.cloned.1.call-update) | async-done | bytes 524304 | tf_op jit(solution)/shard_map/reduce_scatter | solution.py:141
  264.5 2.2 copy.52
  (97 shorter events, 24.8 us)
Async XLA Ops:
  7.2 29.1 %copy-start = (bf16[4,256,1024]{2,1,0:T(8,128)(2,1)S(1)}, bf16[4,256,1024]{2,1,0:T(8,128)(2,1)}, u32[]{:S(2)}) copy-start(bf16[4,256,1024]{2,1,0:T(8,128)(2,1)} %param.12) | copy-start | bytes 6291460
  36.3 3.5 %copy-start.8 = (bf16[8,4,32,256]{3,2,1,0:T(8,128)(2,1)}, bf16[8,4,32,256]{3,2,1,0:T(8,128)(2,1)S(1)}, u32[]{:S(2)}) copy-start(bf16[8,4,32,256]{3,2,1,0:T(8,128)(2,1)S(1)} %all_to_all.20) | copy-start | bytes 1572868
  36.3 3.5 %copy-start.14 = (bf16[4,1024,256]{2,1,0:T(8,128)(2,1)S(1)}, bf16[4,1024,256]{2,1,0:T(8,128)(2,1)}, u32[]{:S(2)}) copy-start(bf16[4,1024,256]{2,1,0:T(8,128)(2,1)} %param.13) | copy-start | bytes 6291460
  39.8 1.3 copy-start.16
  41.1 23.5 %copy-start.11 = (s32[1,512]{1,0:T(1,128)S(1)}, s32[1,512]{1,0:T(1,128)}, u32[]{:S(2)}) copy-start(s32[1,512]{1,0:T(1,128)} %param.16) | copy-start | bytes 6148
  41.1 31.6 %copy-start.13 = (f32[1,512]{1,0:T(1,128)S(1)}, f32[1,512]{1,0:T(1,128)}, u32[]{:S(2)}) copy-start(f32[1,512]{1,0:T(1,128)} %param.15) | copy-start | bytes 6148
  41.1 39.7 %copy-start.12 = (s32[1,2048]{1,0:T(1,128)S(1)}, s32[1,2048]{1,0:T(1,128)}, u32[]{:S(2)}) copy-start(s32[1,2048]{1,0:T(1,128)} %param.17) | copy-start | bytes 24580
  41.1 48.1 %copy-start.5 = (bf16[1,512,256]{2,1,0:T(8,128)(2,1)S(1)}, bf16[1,512,256]{2,1,0:T(8,128)(2,1)}, u32[]{:S(2)}) copy-start(bf16[1,512,256]{2,1,0:T(8,128)(2,1)} %param.14) | copy-start | bytes 786436
  42.0 18.8 %all-to-all-start.1 = ((bf16[8,4,32,256]{3,2,1,0:T(8,128)(2,1)}), bf16[8,4,32,256]{3,2,1,0:T(8,128)(2,1)S(1)}, u32[]{:S(2)}, u32[]{:S(2)}) async-start(bf16[8,4,32,256]{3,2,1,0:T(8,128)(2,1)} %copy.40), calls=%async_computation.1 | async-start | bytes 1048576 | tf_op jit(solution)/shard_map/all_to_all | solution.py:46
  45.5 43.8 %all-gather.7.cloned.1.call-start = ((), (), s32[]{:S(2)}) async-start(), calls=%async_computation.5 | async-start | bytes 1310720 | tf_op jit(solution)/shard_map/all_gather | solution.py:56
  62.8 58.6 %copy-start.2 = (bf16[512,256]{0,1:T(8,128)(2,1)}, bf16[512,256]{0,1:T(8,128)(2,1)S(1)}, u32[]{:S(2)}) copy-start(bf16[512,256]{0,1:T(8,128)(2,1)S(1)} %copy.41) | copy-start | bytes 786436
  63.8 53.8 %all-gather.9.cloned.1.call-start = ((), (), s32[]{:S(2)}) async-start(), calls=%async_computation.7 | async-start | bytes 1310720 | tf_op jit(solution)/shard_map/all_gather | solution.py:96
  64.5 161.9 %all-reduce.3.cloned.1.call-start = ((), (), s32[]{:S(2)}) async-start(), calls=%async_computation.8 | async-start | bytes 4194304
  91.4 26.2 %copy-start.7 = (bf16[512,256]{0,1:T(8,128)(2,1)S(1)}, bf16[512,256]{0,1:T(8,128)(2,1)}, u32[]{:S(2)}) copy-start(bf16[512,256]{0,1:T(8,128)(2,1)} %fusion.80) | copy-start | bytes 786436
  121.4 29.3 %copy-start.4 = (f32[512,256]{0,1:T(8,128)}, f32[512,256]{0,1:T(8,128)S(1)}, u32[]{:S(2)}) copy-start(f32[512,256]{0,1:T(8,128)S(1)} %get-tuple-element.95) | copy-start | bytes 1572868
  144.8 5.9 %copy-start.10 = (bf16[8,4,32,256]{3,2,1,0:T(8,128)(2,1)}, bf16[8,4,32,256]{3,2,1,0:T(8,128)(2,1)S(1)}, u32[]{:S(2)}) copy-start(bf16[8,4,32,256]{3,2,1,0:T(8,128)(2,1)S(1)} %all_to_all.21) | copy-start | bytes 1572868
  144.8 7.3 %copy-start.9 = (bf16[8,4,32,256]{3,2,1,0:T(8,128)(2,1)S(1)}, bf16[8,4,32,256]{3,2,1,0:T(8,128)(2,1)}, u32[]{:S(2)}) copy-start(bf16[8,4,32,256]{3,2,1,0:T(8,128)(2,1)} %copy-done.8) | copy-start | bytes 1572868
  150.7 1.4 copy-start.17
  158.9 4.1 %copy-start.15 = (u32[32]{0:T(128)S(1)}, u32[32]{0:T(128)}, u32[]{:S(2)}) copy-start(u32[32]{0:T(128)} %constant.70) | copy-start | bytes 388
  158.9 5.3 %copy-start.1 = (bf16[2048,256]{0,1:T(8,128)(2,1)S(1)}, bf16[2048,256]{0,1:T(8,128)(2,1)}, u32[]{:S(2)}) copy-start(bf16[2048,256]{0,1:T(8,128)(2,1)} %all-gather.7.cloned.1.call-done) | copy-start | bytes 3145732
  158.9 105.6 %reduce-scatter.2.cloned.1.call-start = ((), (), s32[]{:S(2)}) async-start(), calls=%async_computation.6 | async-start | bytes 2621440 | tf_op jit(solution)/shard_map/reduce_scatter | solution.py:141
  165.5 6.9 %copy-start.6 = (bf16[1,512,256]{2,1,0:T(8,128)(2,1)S(1)}, bf16[1,512,256]{2,1,0:T(8,128)(2,1)}, u32[]{:S(2)}) copy-start(bf16[1,512,256]{2,1,0:T(8,128)(2,1)} %param.14) | copy-start | bytes 786436
  168.7 21.7 %all-to-all-start.3 = ((bf16[8,4,32,256]{3,2,1,0:T(8,128)(2,1)}), bf16[8,4,32,256]{3,2,1,0:T(8,128)(2,1)S(1)}, u32[]{:S(2)}, u32[]{:S(2)}) async-start(bf16[8,4,32,256]{3,2,1,0:T(8,128)(2,1)} %copy.46), calls=%async_computation.3 | async-start | bytes 1048576 | tf_op jit(solution)/shard_map/all_to_all | solution.py:127
  186.5 6.2 %copy-start.3 = (bf16[512,256]{0,1:T(8,128)(2,1)S(1)}, bf16[512,256]{0,1:T(8,128)(2,1)}, u32[]{:S(2)}) copy-start(bf16[512,256]{0,1:T(8,128)(2,1)} %copy-done.2) | copy-start | bytes 786436
Sparse Core Ops, SparseCore 0:
  63.9 25.3 all-gather.6
  91.1 26.4 all-gather.8
  159.0 67.4 all-reduce.2
  229.3 35.1 reduce-scatter.1
where the time goes:
time: 274 us; the launch traced here: 273 us
  waiting for transfers between devices  106 us (39%)
  blocking collectives  65.8 us (24%)
  matrix products  36.9 us (13%)
  local copies, waits for them, and re-layouts  28.4 us (10%)
  between operations  14.8 us (5%)
  other arithmetic  13.4 us (5%)
  starting transfers between devices  7.37 us (3%)
    reduce_scatter x1, waiting for transfers between devices, per_device(): lax.psum_scatter(jnp.einsum('skcr,skcd->rkd', cut_rows, grad_in, preferre...  35.9 us
    unnamed x5, waiting for transfers between devices  30.4 us
    all_to_all x1, blocking collectives, per_device(): lax.all_to_all(scatter_slots(normed), 'expert', split_axis=0, concat_axis...  21.5 us
    all_to_all x1, blocking collectives, per_device(): lax.all_to_all(scatter_slots(grad_low), 'expert', split_axis=0, concat_ax...  19.9 us
    all_gather x1, waiting for transfers between devices, per_device(): all_queries = lax.all_gather(query_matrix, 'dp', axis=0, tiled=True)  16.6 us
    all_to_all x1, waiting for transfers between devices, per_device(): lax.all_to_all(output, 'expert', split_axis=0, concat_axis=0, tiled=True)  15.2 us
    dot_general x4, matrix products, weigh_block(): jnp.einsum('qd,kd->qk', query_matrix, item_tile_rows, preferred_element_t...  8.95 us
    all_gather x1, waiting for transfers between devices, per_device(): shard_rows = lax.all_gather(unit_low, 'dp', axis=0, tiled=True)  8.37 us
  transfers between devices with their start and end apart: 6, of which 5 were waited for; matrix products, arithmetic and copies ran while one was open for 14% of the time, Pallas kernels for 0%

commit v1 on v0

--- a/solution.py
+++ b/solution.py
@@ -2,6 +2,7 @@
 import jax.numpy as jnp
 from jax import lax
 from jax.sharding import PartitionSpec as P
+from jax.lax import axis_index, axis_size, ppermute
 
 CAP = 32
 norm_eps = 1e-06
@@ -10,6 +11,21 @@
 def per_device(
     item_feats, expert_ids, weight_in, weight_out, queries, query_weight, positives, sample_counts
 ):
+
+    def report_gates_up(x_in, k_dim):
+        p_count = axis_size("dp")
+        u_next = sorted(((kk, (kk + 1) % p_count) for kk in range(p_count)))
+        e_now = x_in
+        views = [e_now]
+        for dev in range(1, p_count):
+            e_now = ppermute(e_now, "dp", u_next)
+            views.insert(0, e_now)
+        current_block = jnp.concatenate(views, k_dim)
+        answer = axis_index("dp")
+        tmp = answer + 1
+        carry_in = jnp.roll(current_block, tmp * x_in.shape[k_dim], k_dim)
+        return carry_in
+
     groups = lax.axis_size("expert")
     shards = lax.axis_size("dp")
     local_experts = weight_in.shape[0]
@@ -93,7 +109,7 @@
     grad_queries = jnp.einsum(
         "ira,ias->rs", mixing_factors, block_layout, preferred_element_type=jnp.float32
     )
-    all_queries = lax.all_gather(query_matrix, "dp", axis=0, tiled=True)
+    all_queries = report_gates_up(query_matrix, k_dim=0)
     all_lse, all_weights, all_targets = (
         lax.all_gather(log_total, "dp", axis=0, tiled=True),
         lax.all_gather(weights, "dp", axis=0, tiled=True),

time: 274 us -> 265 us (0.967)
  waiting for transfers between devices: 106 us -> 81.9 us
  local copies, waits for them, and re-layouts: 28.4 us -> 41 us
    all_gather x1 -> x0, waiting for transfers between devices: 16.6 us -> none  [per_device(): all_queries = lax.all_gather(query_matrix, 'dp', axis=0, tiled=True)]
    ppermute x0 -> x3, waiting for transfers between devices: none -> 16.1 us  [report_gates_up(): e_now = ppermute(e_now, 'dp', u_next)]
    all_to_all x1, waiting for transfers between devices: 15.2 us -> 0.01 us  [per_device(): lax.all_to_all(output, 'expert', split_axis=0, concat_axis=0, tiled=True)]
    unnamed x40 -> x53, local copies, waits for them, and re-layouts: 8.16 us -> 18.4 us
    all_gather x1, waiting for transfers between devices: 8.37 us -> 1.37 us  [per_device(): shard_rows = lax.all_gather(unit_low, 'dp', axis=0, tiled=True)]
    unnamed x5 -> x4, waiting for transfers between devices: 30.4 us -> 28.4 us
  transfers between devices with their start and end apart: 6 -> 8, of which waited for: 5 -> 5; matrix products, arithmetic and copies ran while one was open for 14% -> 19% of each run, Pallas kernels for 0% -> 0%
where the time goes in v1:
time: 265 us; the launch traced here: 264 us
  waiting for transfers between devices  81.9 us (31%)
  blocking collectives  66.4 us (25%)
  local copies, waits for them, and re-layouts  41 us (15%)
  matrix products  36.5 us (14%)
  between operations  14.8 us (6%)
  other arithmetic  13.6 us (5%)
  starting transfers between devices  9.47 us (4%)
    reduce_scatter x1, waiting for transfers between devices, per_device(): lax.psum_scatter(jnp.einsum('skcr,skcd->rkd', cut_rows, grad_in, preferre...  36 us
    unnamed x4, waiting for transfers between devices  28.4 us
    all_to_all x1, blocking collectives, per_device(): lax.all_to_all(scatter_slots(normed), 'expert', split_axis=0, concat_axis...  21.5 us
    all_to_all x1, blocking collectives, per_device(): lax.all_to_all(scatter_slots(grad_low), 'expert', split_axis=0, concat_ax...  19.9 us
    unnamed x53, local copies, waits for them, and re-layouts  18.4 us
    ppermute x3, waiting for transfers between devices, report_gates_up(): e_now = ppermute(e_now, 'dp', u_next)  16.1 us
    all_gather x1, blocking collectives, per_device(): lax.all_gather(targets.astype(jnp.float32), 'dp', axis=0, tiled=True)  9.53 us
    dot_general x4, matrix products, weigh_block(): jnp.einsum('qd,kd->qk', query_matrix, item_tile_rows, preferred_element_t...  8.97 us
  transfers between devices with their start and end apart: 8, of which 5 were waited for; matrix products, arithmetic and copies ran while one was open for 19% of the time, Pallas kernels for 0%

profile of v1, /device:TPU:0, one launch (start us, length us, event | category | flops | bytes accessed | tf_op | source)
XLA Modules:
  0.0 263.7 jit_solution(15768600302379769228)
XLA Ops:
  12.3 2.5 scatter_custom_fusion
  14.8 21.5 %all_to_all.20 = bf16[8,4,32,256]{3,2,1,0:T(8,128)(2,1)S(1)} all-to-all(bf16[8,4,32,256]{3,2,1,0:T(8,128)(2,1)S(1)} %bitcast.202), channel_id=1, replica_groups=mesh['dp'=4,'expert'=8] {'expert'}, dimensions={0} | all-to-all | bytes 1048576 | tf_op jit(solution)/shard_map/all_to_all | solution.py:51
  36.3 3.5 %fusion.24 = (bf16[8,4,32,1024]{3,2,0,1:T(8,128)(2,1)S(1)}, f32[4,8,32,1024]{3,2,1,0:T(8,128)}) fusion(bf16[4,256,1024]{2,1,0:T(8,128)(2,1)S(1)} %copy-done, bf16[8,4,32,256]{3,2,1,0:T(8,128)(2,1)S(1)} %all_to_all.20), kind=kOutput, calls=%fused_computation.40 | convolution fusion | flops 546308096 | bytes 8912896 | tf_op jit(solution)/shard_map/skcd,kdf->skcf/dot_general | solution.py:54
  42.0 3.5 %all-to-all-start.1 = ((bf16[8,4,32,256]{3,2,1,0:T(8,128)(2,1)}), bf16[8,4,32,256]{3,2,1,0:T(8,128)(2,1)S(1)}, u32[]{:S(2)}, u32[]{:S(2)}) async-start(bf16[8,4,32,256]{3,2,1,0:T(8,128)(2,1)} %copy.40), calls=%async_computation.1 | async-start | bytes 1048576 | tf_op jit(solution)/shard_map/all_to_all | solution.py:62
  47.1 8.0 %collective-permute-done = bf16[512,256]{1,0:T(8,128)(2,1)S(1)} collective-permute-done((bf16[512,256]{1,0:T(8,128)(2,1)S(1)}, bf16[512,256]{1,0:T(8,128)(2,1)S(1)}, u32[]{:S(2)}, u32[]{:S(2)}) %collective-permute-start) | collective-permute-done | bytes 262176 | tf_op jit(solution)/shard_map/ppermute | solution.py:21
  55.6 8.1 %collective-permute-done.1 = bf16[512,256]{1,0:T(8,128)(2,1)} collective-permute-done((bf16[512,256]{1,0:T(8,128)(2,1)S(1)}, bf16[512,256]{1,0:T(8,128)(2,1)}, u32[]{:S(2)}, u32[]{:S(2)}) %collective-permute-start.1) | collective-permute-done | bytes 262176 | tf_op jit(solution)/shard_map/ppermute | solution.py:21
  63.8 2.6 gather_fusion
  68.6 9.5 %all-gather.2 = f32[4,1,512]{2,1,0:T(1,128)S(1)} all-gather(f32[1,1,512]{2,1,0:T(1,128)S(1)} %bitcast.221), channel_id=1, replica_groups=mesh['dp'=4,'expert'=8] {'dp'}, dimensions={0}, use_global_device_ids=true | all-gather | bytes 10240 | tf_op jit(solution)/shard_map/all_gather | solution.py:116
  78.2 7.2 %all-gather = f32[1,2048]{1,0:T(1,128)S(1)} all-gather(f32[1,512]{1,0:T(1,128)S(1)} %copy-done.16), channel_id=2, replica_groups=mesh['dp'=4,'expert'=8] {'dp'}, dimensions={1}, use_global_device_ids=true | all-gather | bytes 10240 | tf_op jit(solution)/shard_map/all_gather | solution.py:115
  96.4 2.2 subtract_reduce_fusion
  99.9 8.2 %all-gather.1 = f32[4,1,512]{2,1,0:T(1,128)S(1)} all-gather(f32[1,1,512]{2,1,0:T(1,128)S(1)} %bitcast.217), channel_id=1, replica_groups=mesh['dp'=4,'expert'=8] {'dp'}, dimensions={0}, use_global_device_ids=true | all-gather | bytes 10240 | tf_op jit(solution)/shard_map/all_gather | solution.py:114
  108.1 3.6 %multiply_reduce_fusion = (f32[512]{0:T(512)S(1)}, f32[512,256]{0,1:T(8,128)S(1)}) fusion(f32[512]{0:T(512)S(1)} %add_sqrt_fusion, bf16[512,256]{0,1:T(8,128)(2,1)S(1)} %copy.41, bf16[1,512,256]{1,2,0:T(8,128)(2,1)S(1)} %copy.36, bf16[4096,256]{1,0:T(8,128)(2,1)} %constant_dynamic-update-slice_fusion, s32[]{:T(128)S(6)} %select_n.36, ...), kind=kOutput, calls=%fused_computation.77 | convolution fusion | flops 1081867776 | bytes 3441664 | tf_op jit(solution)/shard_map/qk,qd->kd/dot_general | solution.py:129
  112.0 3.1 %scatter_custom_fusion.1 = bf16[1024,256]{1,0:T(8,128)(2,1)} fusion(s32[512]{0:T(512)S(1)} %bitcast.216, bf16[512,256]{1,0:T(8,128)(2,1)S(1)} %copy.44, bf16[]{:T(256)} %constant.33.clone.1), kind=kCustom, calls=%fused_computation.82 | custom fusion | bytes 524290 | tf_op jit(solution)/shard_map/scatter | solution.py:49
  115.2 19.9 %all_to_all.21 = bf16[8,4,32,256]{3,2,1,0:T(8,128)(2,1)S(1)} all-to-all(bf16[8,4,32,256]{3,2,1,0:T(8,128)(2,1)} %bitcast.201), channel_id=1, replica_groups=mesh['dp'=4,'expert'=8] {'expert'}, dimensions={0} | all-to-all | bytes 1048576 | tf_op jit(solution)/shard_map/all_to_all | solution.py:133
  135.1 5.9 %fusion.17 = bf16[8,4,32,1024]{3,2,0,1:T(8,128)(2,1)S(1)} fusion(f32[4,8,32,1024]{3,2,1,0:T(8,128)} %get-tuple-element.91, bf16[4,1024,256]{2,1,0:T(8,128)(2,1)} %param.13, bf16[8,4,32,256]{3,2,1,0:T(8,128)(2,1)S(1)} %all_to_all.21), kind=kOutput, calls=%fused_computation.26 | convolution fusion | flops 557842432 | bytes 8912896 | tf_op jit(solution)/shard_map/skcd,kfd->skcf/dot_general | solution.py:136
  142.4 2.2 fusion.33
  144.6 4.6 %copy.49 = bf16[256,4,1024]{2,1,0:T(4,128)(2,1)} copy(bf16[256,4,1024]{0,2,1:T(8,128)(2,1)} %fusion.33) | data formatting | bytes 4194304 | tf_op jit(solution)/shard_map/convert_element_type | solution.py:151
  150.2 3.7 %fusion.34 = bf16[1024,4,256]{0,2,1:T(8,128)(2,1)} fusion(bf16[8,4,32,256]{3,2,1,0:T(8,128)(2,1)S(1)} %copy-done.13, bf16[8,4,32,1024]{3,2,0,1:T(8,128)(2,1)} %copy-done.19), kind=kOutput, calls=%fused_computation.53 | convolution fusion | flops 537919488 | bytes 4718592 | tf_op jit(solution)/shard_map/skcr,skcd->rkd/dot_general | solution.py:158
  157.2 2.3 fusion.43
  160.3 3.7 %all-to-all-start.3 = ((bf16[8,4,32,256]{3,2,1,0:T(8,128)(2,1)}), bf16[8,4,32,256]{3,2,1,0:T(8,128)(2,1)S(1)}, u32[]{:S(2)}, u32[]{:S(2)}) async-start(bf16[8,4,32,256]{3,2,1,0:T(8,128)(2,1)} %copy.46), calls=%async_computation.3 | async-start | bytes 1048576 | tf_op jit(solution)/shard_map/all_to_all | solution.py:143
  164.1 14.0 %while.10 = (s32[]{:T(128)}, bf16[4,512,512]{1,2,0:T(8,128)(2,1)}, f32[1,512]{1,0:T(1,128)S(1)}, bf16[4,512,256]{2,1,0:T(8,128)(2,1)}, bf16[512,256]{1,0:T(8,128...) while((s32[]{:T(128)}, bf16[4,512,512]{1,2,0:T(8,128)(2,1)}, ...), condition=%wide.region_10.11_spmd, body=%wide.region_9.10_spmd.sunk | while | flops 136053248 | bytes 1066113 | solution.py:106
  165.3 2.2 fusion.95
  168.8 2.2 fusion.95
  172.3 2.3 fusion.95
  175.8 2.2 fusion.95
  178.6 3.4 %convolution_bitcast_fusion = f32[1,512,256]{2,1,0:T(8,128)} fusion(bf16[4,512,512]{1,2,0:T(8,128)(2,1)} %get-tuple-element.52, bf16[4,512,256]{2,1,0:T(8,128)(2,1)} %get-tuple-element.189), kind=kOutput, calls=%fused_computation.58 | convolution fusion | flops 536870912 | bytes 3670016 | tf_op jit(solution)/shard_map/ira,ias->rs/dot_general | solution.py:109
  184.3 2.1 fusion.57
  186.4 2.0 copy.51
  188.4 28.4 %all-reduce.3.cloned.1.call-done = bf16[256,4,1024]{2,1,0:T(4,128)(2,1)} async-done(((bf16[256,4,1024]{2,1,0:T(4,128)(2,1)}), bf16[256,4,1024]{2,1,0:T(4,128)(2,1)}) %all-reduce.3.cloned.1.call-update) | async-done | bytes 2097168
  216.8 2.2 dynamic-slice_convert_fusion
  218.9 36.0 %reduce-scatter.2.cloned.1.call-done = bf16[256,4,256]{0,2,1:T(8,128)(2,1)} async-done(((bf16[1024,4,256]{0,2,1:T(8,128)(2,1)}), bf16[256,4,256]{0,2,1:T(8,128)(2,1)}) %reduce-scatter.2.cloned.1.call-update) | async-done | bytes 524304 | tf_op jit(solution)/shard_map/reduce_scatter | solution.py:157
  255.0 2.2 copy.52
  (114 shorter events, 37.7 us)
Async XLA Ops:
  7.2 29.1 %copy-start = (bf16[4,256,1024]{2,1,0:T(8,128)(2,1)S(1)}, bf16[4,256,1024]{2,1,0:T(8,128)(2,1)}, u32[]{:S(2)}) copy-start(bf16[4,256,1024]{2,1,0:T(8,128)(2,1)} %param.12) | copy-start | bytes 6291460
  36.3 3.5 %copy-start.10 = (bf16[8,4,32,256]{3,2,1,0:T(8,128)(2,1)}, bf16[8,4,32,256]{3,2,1,0:T(8,128)(2,1)S(1)}, u32[]{:S(2)}) copy-start(bf16[8,4,32,256]{3,2,1,0:T(8,128)(2,1)S(1)} %all_to_all.20) | copy-start | bytes 1572868
  36.3 3.5 %copy-start.17 = (bf16[4,1024,256]{2,1,0:T(8,128)(2,1)S(1)}, bf16[4,1024,256]{2,1,0:T(8,128)(2,1)}, u32[]{:S(2)}) copy-start(bf16[4,1024,256]{2,1,0:T(8,128)(2,1)} %param.13) | copy-start | bytes 6291460
  39.8 1.3 copy-start.19
  41.1 4.4 %copy-start.4 = (bf16[1,512,256]{2,1,0:T(8,128)(2,1)S(1)}, bf16[1,512,256]{2,1,0:T(8,128)(2,1)}, u32[]{:S(2)}) copy-start(bf16[1,512,256]{2,1,0:T(8,128)(2,1)} %param.14) | copy-start | bytes 786436
  42.0 21.8 %all-to-all-start.1 = ((bf16[8,4,32,256]{3,2,1,0:T(8,128)(2,1)}), bf16[8,4,32,256]{3,2,1,0:T(8,128)(2,1)S(1)}, u32[]{:S(2)}, u32[]{:S(2)}) async-start(bf16[8,4,32,256]{3,2,1,0:T(8,128)(2,1)} %copy.40), calls=%async_computation.1 | async-start | bytes 1048576 | tf_op jit(solution)/shard_map/all_to_all | solution.py:62
  45.5 50.9 %all-gather.5.cloned.1.call-start = ((), (), s32[]{:S(2)}) async-start(), calls=%async_computation.5 | async-start | bytes 1310720 | tf_op jit(solution)/shard_map/all_gather | solution.py:72
  45.5 9.5 %collective-permute-start = (bf16[512,256]{1,0:T(8,128)(2,1)S(1)}, bf16[512,256]{1,0:T(8,128)(2,1)S(1)}, u32[]{:S(2)}, u32[]{:S(2)}) collective-permute-start(bf16[512,256]{1,0:T(8,128)(2,1)S(1)} %bitcast.199), channel_id=1, source_target_pairs={{0,8},{8,16},{16,24},{24,0},{1,9},{9,17},{17,25},{25,1},{2,10},{10... | collective-permute-start | bytes 786440 | tf_op jit(solution)/shard_map/ppermute | solution.py:21
  55.0 8.7 %copy-start.8 = (bf16[512,256]{1,0:T(8,128)(2,1)}, bf16[512,256]{1,0:T(8,128)(2,1)S(1)}, u32[]{:S(2)}) copy-start(bf16[512,256]{1,0:T(8,128)(2,1)S(1)} %collective-permute-done) | copy-start | bytes 786436
  55.0 8.7 %collective-permute-start.1 = (bf16[512,256]{1,0:T(8,128)(2,1)S(1)}, bf16[512,256]{1,0:T(8,128)(2,1)}, u32[]{:S(2)}, u32[]{:S(2)}) collective-permute-start(bf16[512,256]{1,0:T(8,128)(2,1)S(1)} %collective-permute-done), channel_id=1, source_target_pairs={{0,8},{8,16},{16,24},{24,0},{1,9},{9,17},{17,25},{25,1},{2,10},{10... | collective-permute-start | bytes 786440 | tf_op jit(solution)/shard_map/ppermute | solution.py:21
  63.8 21.7 %collective-permute-start.2 = (bf16[512,256]{1,0:T(8,128)(2,1)}, bf16[512,256]{1,0:T(8,128)(2,1)}, u32[]{:S(2)}, u32[]{:S(2)}) collective-permute-start(bf16[512,256]{1,0:T(8,128)(2,1)} %collective-permute-done.1), channel_id=1, source_target_pairs={{0,8},{8,16},{16,24},{24,0},{1,9},{9,17},{17,25},{25,1},{2,10},{10... | collective-permute-start | bytes 786440 | tf_op jit(solution)/shard_map/ppermute | solution.py:21
  63.8 4.8 %copy-start.15 = (s32[1,2048]{1,0:T(1,128)S(1)}, s32[1,2048]{1,0:T(1,128)}, u32[]{:S(2)}) copy-start(s32[1,2048]{1,0:T(1,128)} %param.17) | copy-start | bytes 24580
  63.8 4.8 %copy-start.14 = (s32[1,512]{1,0:T(1,128)S(1)}, s32[1,512]{1,0:T(1,128)}, u32[]{:S(2)}) copy-start(s32[1,512]{1,0:T(1,128)} %param.16) | copy-start | bytes 6148
  63.8 14.4 %copy-start.16 = (f32[1,512]{1,0:T(1,128)S(1)}, f32[1,512]{1,0:T(1,128)}, u32[]{:S(2)}) copy-start(f32[1,512]{1,0:T(1,128)} %param.15) | copy-start | bytes 6148
  66.4 22.4 %copy-start.9 = (bf16[512,256]{1,0:T(8,128)(2,1)S(1)}, bf16[512,256]{1,0:T(8,128)(2,1)}, u32[]{:S(2)}) copy-start(bf16[512,256]{1,0:T(8,128)(2,1)} %copy-done.8) | copy-start | bytes 786436
  67.5 44.2 %copy-start.2 = (bf16[512,256]{0,1:T(8,128)(2,1)}, bf16[512,256]{0,1:T(8,128)(2,1)S(1)}, u32[]{:S(2)}) copy-start(bf16[512,256]{0,1:T(8,128)(2,1)S(1)} %copy.41) | copy-start | bytes 786436
  68.5 148.3 %all-reduce.3.cloned.1.call-start = ((), (), s32[]{:S(2)}) async-start(), calls=%async_computation.7 | async-start | bytes 4194304
  98.6 9.6 %copy-start.7 = (bf16[512,256]{0,1:T(8,128)(2,1)S(1)}, bf16[512,256]{0,1:T(8,128)(2,1)}, u32[]{:S(2)}) copy-start(bf16[512,256]{0,1:T(8,128)(2,1)} %fusion.78) | copy-start | bytes 786436
  111.7 29.3 %copy-start.6 = (f32[512,256]{0,1:T(8,128)}, f32[512,256]{0,1:T(8,128)S(1)}, u32[]{:S(2)}) copy-start(f32[512,256]{0,1:T(8,128)S(1)} %get-tuple-element.95) | copy-start | bytes 1572868
  135.1 5.9 %copy-start.12 = (bf16[8,4,32,256]{3,2,1,0:T(8,128)(2,1)}, bf16[8,4,32,256]{3,2,1,0:T(8,128)(2,1)S(1)}, u32[]{:S(2)}) copy-start(bf16[8,4,32,256]{3,2,1,0:T(8,128)(2,1)S(1)} %all_to_all.21) | copy-start | bytes 1572868
  135.1 7.3 %copy-start.11 = (bf16[8,4,32,256]{3,2,1,0:T(8,128)(2,1)S(1)}, bf16[8,4,32,256]{3,2,1,0:T(8,128)(2,1)}, u32[]{:S(2)}) copy-start(bf16[8,4,32,256]{3,2,1,0:T(8,128)(2,1)} %copy-done.10) | copy-start | bytes 1572868
  141.0 1.4 copy-start.20
  149.2 1.0 copy-start.13
  149.2 105.7 %reduce-scatter.2.cloned.1.call-start = ((), (), s32[]{:S(2)}) async-start(), calls=%async_computation.6 | async-start | bytes 2621440 | tf_op jit(solution)/shard_map/reduce_scatter | solution.py:157
  153.9 0.7 copy-start.18
  153.9 1.9 copy-start.1
  159.5 4.6 %copy-start.5 = (bf16[1,512,256]{2,1,0:T(8,128)(2,1)S(1)}, bf16[1,512,256]{2,1,0:T(8,128)(2,1)}, u32[]{:S(2)}) copy-start(bf16[1,512,256]{2,1,0:T(8,128)(2,1)} %param.14) | copy-start | bytes 786436
  160.3 21.7 %all-to-all-start.3 = ((bf16[8,4,32,256]{3,2,1,0:T(8,128)(2,1)}), bf16[8,4,32,256]{3,2,1,0:T(8,128)(2,1)S(1)}, u32[]{:S(2)}, u32[]{:S(2)}) async-start(bf16[8,4,32,256]{3,2,1,0:T(8,128)(2,1)} %copy.46), calls=%async_computation.3 | async-start | bytes 1048576 | tf_op jit(solution)/shard_map/all_to_all | solution.py:143
  182.1 2.2 copy-start.3
Sparse Core Ops, SparseCore 0:
  68.6 27.7 all-gather.4
  149.3 67.3 all-reduce.2
  219.7 35.1 reduce-scatter.1
